TPU v7x, 32 devices: a whole 2x2x4 slice. The times are simulated.
32 devices in a mesh: row: 16 (over z, x, core), col: 2 (over y).
Axes of the slice: x: 2, y: 2, z: 4, core: 2. Of those that a mesh axis runs over, the one named last changes fastest.
Arguments:
- features: bfloat16 [4096, 256], P(('row', 'col')), may hold values from -6 to 6
- weight: bfloat16 [256, 256], replicated, may hold values from -0.375 to 0.375
- grad_out: bfloat16 [4096, 256], P(('row', 'col')), may hold values from -6 to 6
- tiles: bfloat16 [16, 2, 24, 128, 128], P('row', 'col'), may hold values from -0.109375 to 0.109375
- slots: int32 [16, 2, 24], P('row', 'col'), may hold values from 0 to 31, as said below
Outputs:
- activated: bfloat16 [4096, 256], P(('row', 'col'))
- grad_weight: float32 [256, 256], replicated
- grad_in: bfloat16 [4096, 256], P(('row', 'col'))
Inputs may be any that keep to these rules, and one draw needn't show every extreme that they name: `slots`: within one tile the 24 entries are distinct.
All inputs are finite; a program needn't handle non-finite values.
Results may differ from a plain program's by a relative error of at most 0.0061.
Values may be sent and summed in bfloat16 or wider, within the bound.
No kernel may reach another device: no remote copies, remote signals or barrier semaphores. Data moves between devices by JAX's collectives and lax.ppermute only.
A program may use at most 128 MiB of HBM per device.

v0:
```python
import math
import jax
import jax.numpy as jnp
from jax import lax
from jax.sharding import PartitionSpec as P


def local(features, weight, grad_out, tiles, slots):
    tile_blocks = tiles[0, 0]
    tile_slots = slots[0, 0]
    own_rows, width = features.shape
    side = tile_blocks.shape[1]
    row_count = lax.axis_size("row")
    col_count = lax.axis_size("col")
    row_blocks = col_count * own_rows // side
    col_blocks = row_count * own_rows // side
    dense_tile = (
        jnp.zeros((row_blocks * col_blocks, side, side), jnp.bfloat16)
        .at[tile_slots]
        .set(tile_blocks)
    )
    dense_tile = dense_tile.reshape(row_blocks, col_blocks, side, side)
    column_panel = lax.all_gather(features, "row", axis=0, tiled=True).reshape(
        col_blocks, side, width
    )
    row_partial = jnp.einsum(
        "bcij,cjf->bif", dense_tile, column_panel, preferred_element_type=jnp.float32
    )
    row_partial = row_partial.reshape(row_blocks * side, width)
    aggregated = lax.psum_scatter(row_partial, "col", scatter_dimension=0, tiled=True).astype(
        jnp.bfloat16
    )
    pre = jnp.dot(aggregated, weight, preferred_element_type=jnp.float32)
    sigmoid_pre = jax.nn.sigmoid(pre)
    activated = (pre * sigmoid_pre).astype(jnp.bfloat16)
    grad_pre = (
        grad_out.astype(jnp.float32) * sigmoid_pre * (1.0 + pre * (1.0 - sigmoid_pre))
    ).astype(jnp.bfloat16)
    weight_term = jnp.dot(aggregated.T, grad_pre, preferred_element_type=jnp.float32)
    total_nodes = own_rows * row_count * col_count
    grad_weight = lax.psum(weight_term, ("row", "col")) * (1.0 / math.sqrt(total_nodes))
    grad_agg = jnp.dot(grad_pre, weight.T, preferred_element_type=jnp.float32).astype(jnp.bfloat16)
    row_panel = lax.all_gather(grad_agg, "col", axis=0, tiled=True).reshape(row_blocks, side, width)
    col_partial = jnp.einsum(
        "bcij,bif->cjf", dense_tile, row_panel, preferred_element_type=jnp.float32
    )
    col_partial = col_partial.reshape(col_blocks * side, width)
    summed = lax.psum_scatter(col_partial, "row", scatter_dimension=0, tiled=True)
    grad_in = summed.astype(jnp.bfloat16)
    return (activated, grad_weight, grad_in)


def solution(mesh):
    in_specs = (
        P(("row", "col"), None),
        P(),
        P(("row", "col"), None),
        P("row", "col", None, None, None),
        P("row", "col", None),
    )
    out_specs = (P(("row", "col"), None), P(), P(("row", "col"), None))
    return jax.shard_map(local, mesh=mesh, in_specs=in_specs, out_specs=out_specs, check_vma=False)
```

profile of v0, /device:TPU:0, one launch (start us, length us, event | category | flops | bytes accessed | tf_op | source)
XLA Modules:
  0.0 269.0 jit_solution(17586135211824430519)
XLA Ops:
  7.2 0.0 copy-start
  7.2 0.0 all-gather.2.cloned.1.call-start
  7.2 0.7 all-gather.2.cloned.1.call-update
  7.9 0.0 reduce-scatter.3.cloned.1.call-start
  8.0 0.7 fusion.4
  8.6 0.2 broadcast_in_dim.4
  8.9 3.5 %scatter_fusion = bf16[32,128,128]{2,1,0:T(8,128)(2,1)S(1)} fusion(bf16[32,128,128]{2,1,0:T(8,128)(2,1)S(1)} %broadcast_in_dim.4, s32[24]{0:T(128)S(1)} %fusion.4, bf16[24,128,128]{2,1,0:T(8,128)(2,1)} %bitcast.29), kind=kCustom, calls=%fused_computation | custom fusion | bytes 2359392 | tf_op jit(solution)/shard_map/scatter | solution.py:20
  12.4 0.1 copy.9
  12.5 38.4 %all-gather.2.cloned.1.call-done = bf16[2048,256]{1,0:T(8,128)(2,1)} async-done(((bf16[128,256]{1,0:T(8,128)(2,1)}), bf16[2048,256]{1,0:T(8,128)(2,1)}) %all-gather.2.cloned.1.call-update) | async-done | bytes 1048592 | tf_op jit(solution)/shard_map/all_gather | solution.py:23
  50.8 2.4 convolution_bitcast_fusion.1
  53.2 0.0 copy-start.1
  53.2 0.0 reduce-scatter.3.cloned.1.call-update
  53.2 0.0 all-reduce.2.cloned.1.call-start
  53.3 0.7 copy.10
  54.0 10.3 %reduce-scatter.3.cloned.1.call-done = f32[128,256]{1,0:T(8,128)} async-done(((f32[256,256]{1,0:T(8,128)}), f32[128,256]{1,0:T(8,128)}) %reduce-scatter.3.cloned.1.call-update) | async-done | bytes 131088 | tf_op jit(solution)/shard_map/reduce_scatter | solution.py:30
  64.3 0.0 copy-done
  64.3 1.7 multiply_convert_fusion.1
  66.0 0.0 copy-done.1
  66.0 0.2 convolution_convert_fusion
  66.2 1.8 fusion
  68.0 0.0 all-reduce.2.cloned.1.call-update
  68.1 0.0 reduce-scatter.5.cloned.1.call-start
  68.1 4.9 %all_gather.7 = bf16[256,256]{1,0:T(8,128)(2,1)S(1)} all-gather(bf16[128,256]{1,0:T(8,128)(2,1)S(1)} %convolution_convert_fusion), channel_id=1, replica_groups=mesh['row'=16,'col'=2] {'col'}, dimensions={0}, use_global_device_ids=true | all-gather | bytes 196608 | tf_op jit(solution)/shard_map/all_gather | solution.py:43
  73.1 1.8 convolution_bitcast_fusion
  74.8 0.0 reduce-scatter.5.cloned.1.call-update
  74.9 121.4 %all-reduce.2.cloned.1.call-done = f32[256,256]{1,0:T(8,128)} async-done(((f32[256,256]{1,0:T(8,128)}), f32[256,256]{1,0:T(8,128)}) %all-reduce.2.cloned.1.call-update) | async-done | bytes 262160 | tf_op jit(solution)/shard_map/psum | solution.py:41
  196.3 1.7 broadcast_multiply_fusion
  197.9 63.0 %reduce-scatter.5.cloned.1.call-done = f32[128,256]{1,0:T(8,128)} async-done(((f32[2048,256]{1,0:T(8,128)}), f32[128,256]{1,0:T(8,128)}) %reduce-scatter.5.cloned.1.call-update) | async-done | bytes 131088 | tf_op jit(solution)/shard_map/reduce_scatter | solution.py:48
  260.9 1.5 convert_element_type.23
Async XLA Ops:
  7.2 57.1 %copy-start = (bf16[256,256]{1,0:T(8,128)(2,1)S(1)}, bf16[256,256]{1,0:T(8,128)(2,1)}, u32[]{:S(2)}) copy-start(bf16[256,256]{1,0:T(8,128)(2,1)} %param.6) | copy-start | bytes 393220
  7.2 43.7 %all-gather.2.cloned.1.call-start = ((), (), s32[]{:S(2)}) async-start(), calls=%async_computation.2 | async-start | bytes 1114112 | tf_op jit(solution)/shard_map/all_gather | solution.py:23
  7.9 56.4 %reduce-scatter.3.cloned.1.call-start = ((), (), s32[]{:S(2)}) async-start(), calls=%async_computation.3 | async-start | bytes 393216 | tf_op jit(solution)/shard_map/reduce_scatter | solution.py:30
  53.2 12.8 %copy-start.1 = (bf16[128,256]{1,0:T(8,128)(2,1)S(1)}, bf16[128,256]{1,0:T(8,128)(2,1)}, u32[]{:S(2)}) copy-start(bf16[128,256]{1,0:T(8,128)(2,1)} %param.7) | copy-start | bytes 196612
  53.2 143.0 %all-reduce.2.cloned.1.call-start = ((), (), s32[]{:S(2)}) async-start(), calls=%async_computation.4 | async-start | bytes 524288 | tf_op jit(solution)/shard_map/psum | solution.py:41
  68.1 192.9 %reduce-scatter.5.cloned.1.call-start = ((), (), s32[]{:S(2)}) async-start(), calls=%async_computation.5 | async-start | bytes 2228224 | tf_op jit(solution)/shard_map/reduce_scatter | solution.py:48
Sparse Core Ops, SparseCore 0:
  10.2 40.6 all-gather.1
  53.6 10.5 reduce-scatter.2
  71.3 124.9 all-reduce.1
  200.3 60.5 reduce-scatter.4
where the time goes:
time: 269 us
  waiting for transfers between devices  234 us (87%)
  between operations  13.8 us (5%)
  matrix products  7.9 us (3%)
  blocking collectives  4.94 us (2%)
  local copies, waits for them, and re-layouts  4.5 us (2%)
  other arithmetic  3.87 us (1%)
    psum x1, waiting for transfers between devices, local(): lax.psum(weight_term, ('row', 'col')) * (1.0 / math.sqrt(total_nodes))  121 us
    reduce_scatter x1, waiting for transfers between devices, local(): lax.psum_scatter(col_partial, 'row', scatter_dimension=0, tiled=True)  63 us
    all_gather x1, waiting for transfers between devices, local(): lax.all_gather(features, 'row', axis=0, tiled=True)  38.4 us
    reduce_scatter x1, waiting for transfers between devices, local(): lax.psum_scatter(row_partial, 'col', scatter_dimension=0, tiled=True)  10.3 us
  transfers between devices with their start and end apart: 4, of which 4 were waited for; matrix products, arithmetic and copies ran while one was open for 3% of the time, Pallas kernels for 0%

commit v1 on v0

--- a/solution.py
+++ b/solution.py
@@ -3,6 +3,10 @@
 import jax.numpy as jnp
 from jax import lax
 from jax.sharding import PartitionSpec as P
+
+
+def convert_vectors(mine, chip_axis, ax_name):
+    return lax.psum(lax.psum(mine, axis_name=chip_axis), axis_name=ax_name)
 
 
 def local(features, weight, grad_out, tiles, slots):
@@ -38,7 +42,7 @@
     ).astype(jnp.bfloat16)
     weight_term = jnp.dot(aggregated.T, grad_pre, preferred_element_type=jnp.float32)
     total_nodes = own_rows * row_count * col_count
-    grad_weight = lax.psum(weight_term, ("row", "col")) * (1.0 / math.sqrt(total_nodes))
+    grad_weight = convert_vectors(weight_term, "col", "row") * (1.0 / math.sqrt(total_nodes))
     grad_agg = jnp.dot(grad_pre, weight.T, preferred_element_type=jnp.float32).astype(jnp.bfloat16)
     row_panel = lax.all_gather(grad_agg, "col", axis=0, tiled=True).reshape(row_blocks, side, width)
     col_partial = jnp.einsum(

time: 269 us -> 257 us (0.955)
  waiting for transfers between devices: 234 us -> 222 us
    psum x1 -> x2, waiting for transfers between devices: 121 us -> 108 us  [convert_vectors(): return lax.psum(lax.psum(mine, axis_name=chip_axis), axis_name=ax_name)]
  transfers between devices with their start and end apart: 4 -> 5, of which waited for: 4 -> 5; matrix products, arithmetic and copies ran while one was open for 3% -> 3% of each run, Pallas kernels for 0% -> 0%
where the time goes in v1:
time: 257 us
  waiting for transfers between devices  222 us (86%)
  between operations  13.8 us (5%)
  matrix products  7.89 us (3%)
  blocking collectives  4.94 us (2%)
  local copies, waits for them, and re-layouts  4.5 us (2%)
  other arithmetic  3.87 us (2%)
    psum x2, waiting for transfers between devices, convert_vectors(): return lax.psum(lax.psum(mine, axis_name=chip_axis), axis_name=ax_name)  108 us
    reduce_scatter x1, waiting for transfers between devices, local(): lax.psum_scatter(col_partial, 'row', scatter_dimension=0, tiled=True)  64 us
    all_gather x1, waiting for transfers between devices, local(): lax.all_gather(features, 'row', axis=0, tiled=True)  38.4 us
    reduce_scatter x1, waiting for transfers between devices, local(): lax.psum_scatter(row_partial, 'col', scatter_dimension=0, tiled=True)  10.3 us
  transfers between devices with their start and end apart: 5, of which 5 were waited for; matrix products, arithmetic and copies ran while one was open for 3% of the time, Pallas kernels for 0%

profile of v1, /device:TPU:0, one launch (start us, length us, event | category | flops | bytes accessed | tf_op | source)
XLA Modules:
  0.0 257.0 jit_solution(1827048118813412140)
XLA Ops:
  7.2 0.0 copy-start
  7.2 0.0 all-gather.2.cloned.1.call-start
  7.2 0.7 all-gather.2.cloned.1.call-update
  7.9 0.0 reduce-scatter.3.cloned.1.call-start
  8.0 0.7 fusion.4
  8.6 0.2 broadcast_in_dim.4
  8.9 3.5 %scatter_fusion = bf16[32,128,128]{2,1,0:T(8,128)(2,1)S(1)} fusion(bf16[32,128,128]{2,1,0:T(8,128)(2,1)S(1)} %broadcast_in_dim.4, s32[24]{0:T(128)S(1)} %fusion.4, bf16[24,128,128]{2,1,0:T(8,128)(2,1)} %bitcast.29), kind=kCustom, calls=%fused_computation | custom fusion | bytes 2359392 | tf_op jit(solution)/shard_map/scatter | solution.py:24
  12.4 0.1 copy.9
  12.5 38.4 %all-gather.2.cloned.1.call-done = bf16[2048,256]{1,0:T(8,128)(2,1)} async-done(((bf16[128,256]{1,0:T(8,128)(2,1)}), bf16[2048,256]{1,0:T(8,128)(2,1)}) %all-gather.2.cloned.1.call-update) | async-done | bytes 1048592 | tf_op jit(solution)/shard_map/all_gather | solution.py:27
  50.8 2.4 convolution_bitcast_fusion.1
  53.2 0.0 copy-start.1
  53.2 0.0 reduce-scatter.3.cloned.1.call-update
  53.2 0.0 all-reduce.3.cloned.1.call-start
  53.3 0.7 copy.10
  54.0 10.3 %reduce-scatter.3.cloned.1.call-done = f32[128,256]{1,0:T(8,128)} async-done(((f32[256,256]{1,0:T(8,128)}), f32[128,256]{1,0:T(8,128)}) %reduce-scatter.3.cloned.1.call-update) | async-done | bytes 131088 | tf_op jit(solution)/shard_map/reduce_scatter | solution.py:34
  64.3 0.0 copy-done
  64.3 1.7 multiply_convert_fusion.1
  66.0 0.0 copy-done.1
  66.0 1.8 fusion
  67.8 0.0 all-reduce.3.cloned.1.call-update
  67.9 0.0 all-reduce.5.cloned.1.call-start
  67.9 0.2 convolution_convert_fusion
  68.1 4.9 %all_gather.7 = bf16[256,256]{1,0:T(8,128)(2,1)S(1)} all-gather(bf16[128,256]{1,0:T(8,128)(2,1)S(1)} %convolution_convert_fusion), channel_id=1, replica_groups=mesh['row'=16,'col'=2] {'col'}, dimensions={0}, use_global_device_ids=true | all-gather | bytes 196608 | tf_op jit(solution)/shard_map/all_gather | solution.py:47
  73.1 18.2 %all-reduce.3.cloned.1.call-done = f32[256,256]{1,0:T(8,128)} async-done(((f32[256,256]{1,0:T(8,128)}), f32[256,256]{1,0:T(8,128)}) %all-reduce.3.cloned.1.call-update) | async-done | bytes 262160 | tf_op jit(solution)/shard_map/psum | solution.py:9
  91.2 0.0 all-reduce.5.cloned.1.call-update
  91.2 0.0 reduce-scatter.5.cloned.1.call-start
  91.3 1.8 convolution_bitcast_fusion
  93.0 0.0 reduce-scatter.5.cloned.1.call-update
  93.1 90.2 %all-reduce.5.cloned.1.call-done = f32[256,256]{1,0:T(8,128)} async-done(((f32[256,256]{1,0:T(8,128)}), f32[256,256]{1,0:T(8,128)}) %all-reduce.5.cloned.1.call-update) | async-done | bytes 262160 | tf_op jit(solution)/shard_map/psum | solution.py:9
  183.2 1.7 broadcast_multiply_fusion
  184.9 64.0 %reduce-scatter.5.cloned.1.call-done = f32[128,256]{1,0:T(8,128)} async-done(((f32[2048,256]{1,0:T(8,128)}), f32[128,256]{1,0:T(8,128)}) %reduce-scatter.5.cloned.1.call-update) | async-done | bytes 131088 | tf_op jit(solution)/shard_map/reduce_scatter | solution.py:52
  248.9 1.5 convert_element_type.23
Async XLA Ops:
  7.2 57.1 %copy-start = (bf16[256,256]{1,0:T(8,128)(2,1)S(1)}, bf16[256,256]{1,0:T(8,128)(2,1)}, u32[]{:S(2)}) copy-start(bf16[256,256]{1,0:T(8,128)(2,1)} %param.6) | copy-start | bytes 393220
  7.2 43.7 %all-gather.2.cloned.1.call-start = ((), (), s32[]{:S(2)}) async-start(), calls=%async_computation.2 | async-start | bytes 1114112 | tf_op jit(solution)/shard_map/all_gather | solution.py:27
  7.9 56.4 %reduce-scatter.3.cloned.1.call-start = ((), (), s32[]{:S(2)}) async-start(), calls=%async_computation.3 | async-start | bytes 393216 | tf_op jit(solution)/shard_map/reduce_scatter | solution.py:34
  53.2 12.8 %copy-start.1 = (bf16[128,256]{1,0:T(8,128)(2,1)S(1)}, bf16[128,256]{1,0:T(8,128)(2,1)}, u32[]{:S(2)}) copy-start(bf16[128,256]{1,0:T(8,128)(2,1)} %param.7) | copy-start | bytes 196612
  53.2 38.0 %all-reduce.3.cloned.1.call-start = ((), (), s32[]{:S(2)}) async-start(), calls=%async_computation.4 | async-start | bytes 524288 | tf_op jit(solution)/shard_map/psum | solution.py:9
  67.9 115.4 %all-reduce.5.cloned.1.call-start = ((), (), s32[]{:S(2)}) async-start(), calls=%async_computation.5 | async-start | bytes 524288 | tf_op jit(solution)/shard_map/psum | solution.py:9
  91.2 157.7 %reduce-scatter.5.cloned.1.call-start = ((), (), s32[]{:S(2)}) async-start(), calls=%async_computation.6 | async-start | bytes 2228224 | tf_op jit(solution)/shard_map/reduce_scatter | solution.py:52
Sparse Core Ops, SparseCore 0:
  10.2 40.6 all-gather.1
  53.6 10.5 reduce-scatter.2
  68.0 23.1 all-reduce.2
  94.5 88.7 all-reduce.4
  186.8 62.0 reduce-scatter.4
